TPU v7x, 32 devices: a whole 2x2x4 slice. The times are simulated.
32 devices in a mesh: con: 16 (over z, y, x), rep: 2 (over core).
Axes of the slice: x: 2, y: 2, z: 4, core: 2. Of those that a mesh axis runs over, the one named last changes fastest.
Arguments:
- tamps: bfloat16 [16384, 14336], P('rep', 'con'), may hold values from -6 to 6
- integrals: bfloat16 [1024, 16384], P('con', 'rep'), may hold values from -0.0625 to 0.0625
Outputs:
- ladder: bfloat16 [1024, 14336], P('rep', 'con')
All inputs are finite; a program needn't handle non-finite values.
Results may differ from a plain program's by a relative error of at most 0.001.
Values may be sent and summed in bfloat16 or wider, within the bound.
A program may use at most 128 MiB of HBM per device.

v0:
```python
import jax
import jax.numpy as jnp
from jax import lax
from jax.sharding import PartitionSpec as P


def shards(tamps, integrals):
    gathered = lax.all_gather(integrals, "con", axis=0, tiled=True)
    partial_value = jnp.dot(gathered, tamps, preferred_element_type=jnp.float32)
    summed = lax.psum_scatter(partial_value, "rep", scatter_dimension=0, tiled=True)
    return summed.astype(jnp.bfloat16)


def solution(mesh):
    in_specs = (P("rep", "con"), P("con", "rep"))
    out_specs = P("rep", "con")
    return jax.shard_map(shards, mesh=mesh, in_specs=in_specs, out_specs=out_specs, check_vma=False)
```

profile of v0, /device:TPU:0, one launch (start us, length us, event | category | flops | bytes accessed | tf_op | source)
XLA Modules:
  0.0 246.8 jit_solution(9029354542625471517)
XLA Ops:
  6.5 0.0 all-gather.2.cloned.1.call-start
  6.5 0.7 all-gather.2.cloned.1.call-update
  7.3 0.0 reduce-scatter.2.cloned.1.call-start
  7.3 197.2 %all-gather.2.cloned.1.call-done = bf16[1024,8192]{1,0:T(8,128)(2,1)} async-done(((bf16[64,8192]{1,0:T(8,128)(2,1)}), bf16[1024,8192]{1,0:T(8,128)(2,1)}) %all-gather.2.cloned.1.call-update) | async-done | bytes 16777232 | tf_op jit(solution)/shard_map/all_gather | solution.py:8
  204.5 23.1 %fusion = f32[1024,896]{1,0:T(8,128)} fusion(bf16[1024,8192]{1,0:T(8,128)(2,1)} %all-gather.2.cloned.1.call-done, bf16[8192,896]{1,0:T(8,128)(2,1)} %param.2), kind=kOutput, calls=%fused_computation | convolution fusion | flops 15032385536 | bytes 35127296 | tf_op jit(solution)/shard_map/dot_general | solution.py:9
  227.6 0.0 reduce-scatter.2.cloned.1.call-update
  227.6 9.9 %reduce-scatter.2.cloned.1.call-done = f32[512,896]{1,0:T(8,128)} async-done(((f32[1024,896]{1,0:T(8,128)}), f32[512,896]{1,0:T(8,128)}) %reduce-scatter.2.cloned.1.call-update) | async-done | bytes 1835024 | tf_op jit(solution)/shard_map/reduce_scatter | solution.py:10
  237.5 2.5 %convert_element_type.3 = bf16[512,896]{1,0:T(8,128)(2,1)} convert(f32[512,896]{1,0:T(8,128)} %reduce-scatter.2.cloned.1.call-done) | non-fusion elementwise | flops 458752 | bytes 2752512 | tf_op jit(solution)/shard_map/convert_element_type | solution.py:11
Async XLA Ops:
  6.5 197.9 %all-gather.2.cloned.1.call-start = ((), (), s32[]{:S(2)}) async-start(), calls=%async_computation.1 | async-start | bytes 17825792 | tf_op jit(solution)/shard_map/all_gather | solution.py:8
  7.3 230.2 %reduce-scatter.2.cloned.1.call-start = ((), (), s32[]{:S(2)}) async-start(), calls=%async_computation.2 | async-start | bytes 5505024 | tf_op jit(solution)/shard_map/reduce_scatter | solution.py:10
Sparse Core Ops, SparseCore 0:
  10.1 194.3 all-gather.1
  227.7 9.7 reduce-scatter.1
where the time goes:
time: 247 us
  waiting for transfers between devices  208 us (84%)
  matrix products  23.1 us (9%)
  between operations  13.4 us (5%)
  other arithmetic  2.52 us (1%)
    all_gather x1, waiting for transfers between devices, shards(): gathered = lax.all_gather(integrals, 'con', axis=0, tiled=True)  197 us
    dot_general x1, matrix products, shards(): partial_value = jnp.dot(gathered, tamps, preferred_element_type=jnp.float32)  23.1 us
    reduce_scatter x1, waiting for transfers between devices, shards(): lax.psum_scatter(partial_value, 'rep', scatter_dimension=0, tiled=True)  9.87 us
  transfers between devices with their start and end apart: 2, of which 2 were waited for; matrix products, arithmetic and copies ran while one was open for 0% of the time, Pallas kernels for 0%

commit v1 on v0

--- a/solution.py
+++ b/solution.py
@@ -4,8 +4,22 @@
 from jax.sharding import PartitionSpec as P
 
 
+def _perform_stops_all(u_in, d0):
+    world = jax.lax.axis_size("con")
+    part_next = u_in
+    rack = [part_next]
+    back = sorted(((c, (c + 1) % world) for c in range(world)))
+    for kk in range(1, world):
+        part_next = jax.lax.ppermute(part_next, "con", back)
+        rack.insert(0, part_next)
+    z1 = jnp.roll(
+        jnp.concatenate(rack, axis=d0), (jax.lax.axis_index("con") + 1) * u_in.shape[d0], axis=d0
+    )
+    return z1
+
+
 def shards(tamps, integrals):
-    gathered = lax.all_gather(integrals, "con", axis=0, tiled=True)
+    gathered = _perform_stops_all(integrals, 0)
     partial_value = jnp.dot(gathered, tamps, preferred_element_type=jnp.float32)
     summed = lax.psum_scatter(partial_value, "rep", scatter_dimension=0, tiled=True)
     return summed.astype(jnp.bfloat16)

time: 247 us -> 473 us (1.91)
  waiting for transfers between devices: 208 us -> 367 us
  local copies, waits for them, and re-layouts: 0 us -> 64.6 us
    ppermute x0 -> x15, waiting for transfers between devices: none -> 359 us  [_perform_stops_all(): part_next = jax.lax.ppermute(part_next, 'con', back)]
    all_gather x1 -> x0, waiting for transfers between devices: 197 us -> none  [shards(): gathered = lax.all_gather(integrals, 'con', axis=0, tiled=True)]
    unnamed x0 -> x85, local copies, waits for them, and re-layouts: none -> 63.5 us
  transfers between devices with their start and end apart: 2 -> 16, of which waited for: 2 -> 16; matrix products, arithmetic and copies ran while one was open for 0% -> 0% of each run, Pallas kernels for 0% -> 0%
where the time goes in v1:
time: 473 us; the launch traced here: 472 us
  waiting for transfers between devices  367 us (78%)
  local copies, waits for them, and re-layouts  64.6 us (14%)
  matrix products  21.7 us (5%)
  between operations  13.5 us (3%)
    ppermute x15, waiting for transfers between devices, _perform_stops_all(): part_next = jax.lax.ppermute(part_next, 'con', back)  359 us
    unnamed x85, local copies, waits for them, and re-layouts  63.5 us
    dot_general x1, matrix products, shards(): partial_value = jnp.dot(gathered, tamps, preferred_element_type=jnp.float32)  21.7 us
  transfers between devices with their start and end apart: 16, of which 16 were waited for; matrix products, arithmetic and copies ran while one was open for 0% of the time, Pallas kernels for 0%

profile of v1, /device:TPU:0, one launch (start us, length us, event | category | flops | bytes accessed | tf_op | source)
XLA Modules:
  0.0 472.2 jit_solution(28112321083097697)
XLA Ops:
  6.5 2.9 collective-permute-start
  9.5 27.4 %collective-permute-done = bf16[64,8192]{1,0:T(8,128)(2,1)S(1)} collective-permute-done((bf16[64,8192]{1,0:T(8,128)(2,1)}, bf16[64,8192]{1,0:T(8,128)(2,1)S(1)}, u32[]{:S(2)}, u32[]{:S(2)}) %collective-permute-start) | collective-permute-done | bytes 1048608 | tf_op jit(solution)/shard_map/ppermute | solution.py:13
  36.9 27.9 %collective-permute-done.1 = bf16[64,8192]{1,0:T(8,128)(2,1)S(1)} collective-permute-done((bf16[64,8192]{1,0:T(8,128)(2,1)S(1)}, bf16[64,8192]{1,0:T(8,128)(2,1)S(1)}, u32[]{:S(2)}, u32[]{:S(2)}) %collective-permute-start.1) | collective-permute-done | bytes 1048608 | tf_op jit(solution)/shard_map/ppermute | solution.py:13
  64.9 27.0 %collective-permute-done.2 = bf16[64,8192]{1,0:T(8,128)(2,1)S(1)} collective-permute-done((bf16[64,8192]{1,0:T(8,128)(2,1)S(1)}, bf16[64,8192]{1,0:T(8,128)(2,1)S(1)}, u32[]{:S(2)}, u32[]{:S(2)}) %collective-permute-start.2) | collective-permute-done | bytes 1048608 | tf_op jit(solution)/shard_map/ppermute | solution.py:13
  92.8 26.1 %collective-permute-done.3 = bf16[64,8192]{1,0:T(8,128)(2,1)S(1)} collective-permute-done((bf16[64,8192]{1,0:T(8,128)(2,1)S(1)}, bf16[64,8192]{1,0:T(8,128)(2,1)S(1)}, u32[]{:S(2)}, u32[]{:S(2)}) %collective-permute-start.3) | collective-permute-done | bytes 1048608 | tf_op jit(solution)/shard_map/ppermute | solution.py:13
  119.9 25.2 %collective-permute-done.4 = bf16[64,8192]{1,0:T(8,128)(2,1)S(1)} collective-permute-done((bf16[64,8192]{1,0:T(8,128)(2,1)S(1)}, bf16[64,8192]{1,0:T(8,128)(2,1)S(1)}, u32[]{:S(2)}, u32[]{:S(2)}) %collective-permute-start.4) | collective-permute-done | bytes 1048608 | tf_op jit(solution)/shard_map/ppermute | solution.py:13
  146.1 24.3 %collective-permute-done.5 = bf16[64,8192]{1,0:T(8,128)(2,1)S(1)} collective-permute-done((bf16[64,8192]{1,0:T(8,128)(2,1)S(1)}, bf16[64,8192]{1,0:T(8,128)(2,1)S(1)}, u32[]{:S(2)}, u32[]{:S(2)}) %collective-permute-start.5) | collective-permute-done | bytes 1048608 | tf_op jit(solution)/shard_map/ppermute | solution.py:13
  171.3 23.3 %collective-permute-done.6 = bf16[64,8192]{1,0:T(8,128)(2,1)S(1)} collective-permute-done((bf16[64,8192]{1,0:T(8,128)(2,1)S(1)}, bf16[64,8192]{1,0:T(8,128)(2,1)S(1)}, u32[]{:S(2)}, u32[]{:S(2)}) %collective-permute-start.6) | collective-permute-done | bytes 1048608 | tf_op jit(solution)/shard_map/ppermute | solution.py:13
  195.7 22.4 %collective-permute-done.7 = bf16[64,8192]{1,0:T(8,128)(2,1)S(1)} collective-permute-done((bf16[64,8192]{1,0:T(8,128)(2,1)S(1)}, bf16[64,8192]{1,0:T(8,128)(2,1)S(1)}, u32[]{:S(2)}, u32[]{:S(2)}) %collective-permute-start.7) | collective-permute-done | bytes 1048608 | tf_op jit(solution)/shard_map/ppermute | solution.py:13
  219.1 22.4 %collective-permute-done.8 = bf16[64,8192]{1,0:T(8,128)(2,1)S(1)} collective-permute-done((bf16[64,8192]{1,0:T(8,128)(2,1)S(1)}, bf16[64,8192]{1,0:T(8,128)(2,1)S(1)}, u32[]{:S(2)}, u32[]{:S(2)}) %collective-permute-start.8) | collective-permute-done | bytes 1048608 | tf_op jit(solution)/shard_map/ppermute | solution.py:13
  242.4 22.3 %collective-permute-done.9 = bf16[64,8192]{1,0:T(8,128)(2,1)S(1)} collective-permute-done((bf16[64,8192]{1,0:T(8,128)(2,1)S(1)}, bf16[64,8192]{1,0:T(8,128)(2,1)S(1)}, u32[]{:S(2)}, u32[]{:S(2)}) %collective-permute-start.9) | collective-permute-done | bytes 1048608 | tf_op jit(solution)/shard_map/ppermute | solution.py:13
  265.7 22.3 %collective-permute-done.10 = bf16[64,8192]{1,0:T(8,128)(2,1)S(1)} collective-permute-done((bf16[64,8192]{1,0:T(8,128)(2,1)S(1)}, bf16[64,8192]{1,0:T(8,128)(2,1)S(1)}, u32[]{:S(2)}, u32[]{:S(2)}) %collective-permute-start.10) | collective-permute-done | bytes 1048608 | tf_op jit(solution)/shard_map/ppermute | solution.py:13
  289.1 22.4 %collective-permute-done.11 = bf16[64,8192]{1,0:T(8,128)(2,1)S(1)} collective-permute-done((bf16[64,8192]{1,0:T(8,128)(2,1)S(1)}, bf16[64,8192]{1,0:T(8,128)(2,1)S(1)}, u32[]{:S(2)}, u32[]{:S(2)}) %collective-permute-start.11) | collective-permute-done | bytes 1048608 | tf_op jit(solution)/shard_map/ppermute | solution.py:13
  312.4 22.9 %collective-permute-done.12 = bf16[64,8192]{1,0:T(8,128)(2,1)S(1)} collective-permute-done((bf16[64,8192]{1,0:T(8,128)(2,1)S(1)}, bf16[64,8192]{1,0:T(8,128)(2,1)S(1)}, u32[]{:S(2)}, u32[]{:S(2)}) %collective-permute-start.12) | collective-permute-done | bytes 1048608 | tf_op jit(solution)/shard_map/ppermute | solution.py:13
  336.3 24.7 %collective-permute-done.13 = bf16[64,8192]{1,0:T(8,128)(2,1)} collective-permute-done((bf16[64,8192]{1,0:T(8,128)(2,1)S(1)}, bf16[64,8192]{1,0:T(8,128)(2,1)}, u32[]{:S(2)}, u32[]{:S(2)}) %collective-permute-start.13) | collective-permute-done | bytes 1048608 | tf_op jit(solution)/shard_map/ppermute | solution.py:13
  361.1 18.6 %collective-permute-done.14 = bf16[64,8192]{1,0:T(8,128)(2,1)} collective-permute-done((bf16[64,8192]{1,0:T(8,128)(2,1)}, bf16[64,8192]{1,0:T(8,128)(2,1)}, u32[]{:S(2)}, u32[]{:S(2)}) %collective-permute-start.14) | collective-permute-done | bytes 1048608 | tf_op jit(solution)/shard_map/ppermute | solution.py:13
  379.7 2.3 constant_dynamic-update-slice_fusion.31
  382.0 2.3 constant_dynamic-update-slice_fusion.30
  384.3 2.3 constant_dynamic-update-slice_fusion.29
  386.5 2.3 constant_dynamic-update-slice_fusion.28
  388.8 2.3 constant_dynamic-update-slice_fusion.27
  391.1 2.3 constant_dynamic-update-slice_fusion.26
  393.4 2.3 constant_dynamic-update-slice_fusion.25
  395.7 2.3 constant_dynamic-update-slice_fusion.24
  398.0 2.4 constant_dynamic-update-slice_fusion.23
  400.4 2.3 constant_dynamic-update-slice_fusion.22
  402.7 2.3 constant_dynamic-update-slice_fusion.21
  404.9 2.3 constant_dynamic-update-slice_fusion.20
  407.2 2.3 constant_dynamic-update-slice_fusion.19
  410.5 1.1 constant_dynamic-update-slice_fusion.17
  411.6 2.3 constant_dynamic-update-slice_fusion.16
  413.9 2.5 constant_dynamic-update-slice_fusion.15
  416.3 2.3 constant_dynamic-update-slice_fusion.14
  418.6 1.0 constant_dynamic-update-slice_fusion.13
  419.6 1.1 constant_dynamic-update-slice_fusion.12
  420.7 1.1 constant_dynamic-update-slice_fusion.11
  421.8 1.1 constant_dynamic-update-slice_fusion.10
  423.9 1.1 constant_dynamic-update-slice_fusion.8
  425.0 1.0 constant_dynamic-update-slice_fusion.7
  426.1 1.0 constant_dynamic-update-slice_fusion.6
  427.1 1.0 constant_dynamic-update-slice_fusion.5
  428.2 1.1 constant_dynamic-update-slice_fusion.4
  429.3 1.0 constant_dynamic-update-slice_fusion.3
  431.3 1.1 constant_dynamic-update-slice_fusion.1
  432.4 1.1 constant_dynamic-update-slice_fusion
  433.5 21.7 %fusion = f32[1024,896]{1,0:T(8,128)} fusion(bf16[8192,896]{1,0:T(8,128)(2,1)S(1)} %bitcast.2, bf16[2048,8192]{1,0:T(8,128)(2,1)} %constant_dynamic-update-slice_fusion, s32[]{:T(128)S(6)} %select_n.14), kind=kOutput, calls=%fused_computation | convolution fusion | flops 15032385536 | bytes 35127300 | tf_op jit(solution)/shard_map/dot_general | solution.py:23
  455.2 7.6 %reduce-scatter.2.cloned.1.call-done = f32[512,896]{1,0:T(8,128)} async-done(((f32[1024,896]{1,0:T(8,128)}), f32[512,896]{1,0:T(8,128)}) %reduce-scatter.2.cloned.1.call-update) | async-done | bytes 1835024 | tf_op jit(solution)/shard_map/reduce_scatter | solution.py:24
  462.8 2.5 convert_element_type.3
  (74 shorter events, 14.0 us)
Async XLA Ops:
  6.5 425.9 %copy-start = (bf16[64,8192]{1,0:T(8,128)(2,1)S(1)}, bf16[64,8192]{1,0:T(8,128)(2,1)}, u32[]{:S(2)}) copy-start(bf16[64,8192]{1,0:T(8,128)(2,1)} %param.3) | copy-start | bytes 3145732
  6.5 456.3 %reduce-scatter.2.cloned.1.call-start = ((), (), s32[]{:S(2)}) async-start(), calls=%async_computation.1 | async-start | bytes 5505024 | tf_op jit(solution)/shard_map/reduce_scatter | solution.py:24
  6.5 30.4 %collective-permute-start = (bf16[64,8192]{1,0:T(8,128)(2,1)}, bf16[64,8192]{1,0:T(8,128)(2,1)S(1)}, u32[]{:S(2)}, u32[]{:S(2)}) collective-permute-start(bf16[64,8192]{1,0:T(8,128)(2,1)} %param.3), channel_id=1, source_target_pairs={{0,2},{2,4},{4,6},{6,8},{8,10},{10,12},{12,14},{14,16},{16,18},{18... | collective-permute-start | bytes 3145736 | tf_op jit(solution)/shard_map/ppermute | solution.py:13
  36.9 27.9 %collective-permute-start.1 = (bf16[64,8192]{1,0:T(8,128)(2,1)S(1)}, bf16[64,8192]{1,0:T(8,128)(2,1)S(1)}, u32[]{:S(2)}, u32[]{:S(2)}) collective-permute-start(bf16[64,8192]{1,0:T(8,128)(2,1)S(1)} %collective-permute-done), channel_id=1, source_target_pairs={{0,2},{2,4},{4,6},{6,8},{8,10},{10,12},{12,14},{14,16},{16,18},{18... | collective-permute-start | bytes 3145736 | tf_op jit(solution)/shard_map/ppermute | solution.py:13
  64.8 27.0 %collective-permute-start.2 = (bf16[64,8192]{1,0:T(8,128)(2,1)S(1)}, bf16[64,8192]{1,0:T(8,128)(2,1)S(1)}, u32[]{:S(2)}, u32[]{:S(2)}) collective-permute-start(bf16[64,8192]{1,0:T(8,128)(2,1)S(1)} %collective-permute-done.1), channel_id=1, source_target_pairs={{0,2},{2,4},{4,6},{6,8},{8,10},{10,12},{12,14},{14,16},{16,18},{18... | collective-permute-start | bytes 3145736 | tf_op jit(solution)/shard_map/ppermute | solution.py:13
  91.9 1.0 copy-start.1
  92.8 26.1 %collective-permute-start.3 = (bf16[64,8192]{1,0:T(8,128)(2,1)S(1)}, bf16[64,8192]{1,0:T(8,128)(2,1)S(1)}, u32[]{:S(2)}, u32[]{:S(2)}) collective-permute-start(bf16[64,8192]{1,0:T(8,128)(2,1)S(1)} %collective-permute-done.2), channel_id=1, source_target_pairs={{0,2},{2,4},{4,6},{6,8},{8,10},{10,12},{12,14},{14,16},{16,18},{18... | collective-permute-start | bytes 3145736 | tf_op jit(solution)/shard_map/ppermute | solution.py:13
  118.9 1.0 copy-start.3
  119.9 25.2 %collective-permute-start.4 = (bf16[64,8192]{1,0:T(8,128)(2,1)S(1)}, bf16[64,8192]{1,0:T(8,128)(2,1)S(1)}, u32[]{:S(2)}, u32[]{:S(2)}) collective-permute-start(bf16[64,8192]{1,0:T(8,128)(2,1)S(1)} %collective-permute-done.3), channel_id=1, source_target_pairs={{0,2},{2,4},{4,6},{6,8},{8,10},{10,12},{12,14},{14,16},{16,18},{18... | collective-permute-start | bytes 3145736 | tf_op jit(solution)/shard_map/ppermute | solution.py:13
  145.1 1.0 copy-start.5
  146.1 24.3 %collective-permute-start.5 = (bf16[64,8192]{1,0:T(8,128)(2,1)S(1)}, bf16[64,8192]{1,0:T(8,128)(2,1)S(1)}, u32[]{:S(2)}, u32[]{:S(2)}) collective-permute-start(bf16[64,8192]{1,0:T(8,128)(2,1)S(1)} %collective-permute-done.4), channel_id=1, source_target_pairs={{0,2},{2,4},{4,6},{6,8},{8,10},{10,12},{12,14},{14,16},{16,18},{18... | collective-permute-start | bytes 3145736 | tf_op jit(solution)/shard_map/ppermute | solution.py:13
  170.3 1.0 copy-start.7
  171.3 23.3 %collective-permute-start.6 = (bf16[64,8192]{1,0:T(8,128)(2,1)S(1)}, bf16[64,8192]{1,0:T(8,128)(2,1)S(1)}, u32[]{:S(2)}, u32[]{:S(2)}) collective-permute-start(bf16[64,8192]{1,0:T(8,128)(2,1)S(1)} %collective-permute-done.5), channel_id=1, source_target_pairs={{0,2},{2,4},{4,6},{6,8},{8,10},{10,12},{12,14},{14,16},{16,18},{18... | collective-permute-start | bytes 3145736 | tf_op jit(solution)/shard_map/ppermute | solution.py:13
  194.7 1.0 copy-start.9
  195.7 22.4 %collective-permute-start.7 = (bf16[64,8192]{1,0:T(8,128)(2,1)S(1)}, bf16[64,8192]{1,0:T(8,128)(2,1)S(1)}, u32[]{:S(2)}, u32[]{:S(2)}) collective-permute-start(bf16[64,8192]{1,0:T(8,128)(2,1)S(1)} %collective-permute-done.6), channel_id=1, source_target_pairs={{0,2},{2,4},{4,6},{6,8},{8,10},{10,12},{12,14},{14,16},{16,18},{18... | collective-permute-start | bytes 3145736 | tf_op jit(solution)/shard_map/ppermute | solution.py:13
  218.1 1.0 copy-start.11
  219.1 22.4 %collective-permute-start.8 = (bf16[64,8192]{1,0:T(8,128)(2,1)S(1)}, bf16[64,8192]{1,0:T(8,128)(2,1)S(1)}, u32[]{:S(2)}, u32[]{:S(2)}) collective-permute-start(bf16[64,8192]{1,0:T(8,128)(2,1)S(1)} %collective-permute-done.7), channel_id=1, source_target_pairs={{0,2},{2,4},{4,6},{6,8},{8,10},{10,12},{12,14},{14,16},{16,18},{18... | collective-permute-start | bytes 3145736 | tf_op jit(solution)/shard_map/ppermute | solution.py:13
  241.4 1.0 copy-start.13
  242.4 22.3 %collective-permute-start.9 = (bf16[64,8192]{1,0:T(8,128)(2,1)S(1)}, bf16[64,8192]{1,0:T(8,128)(2,1)S(1)}, u32[]{:S(2)}, u32[]{:S(2)}) collective-permute-start(bf16[64,8192]{1,0:T(8,128)(2,1)S(1)} %collective-permute-done.8), channel_id=1, source_target_pairs={{0,2},{2,4},{4,6},{6,8},{8,10},{10,12},{12,14},{14,16},{16,18},{18... | collective-permute-start | bytes 3145736 | tf_op jit(solution)/shard_map/ppermute | solution.py:13
  264.7 1.0 copy-start.15
  265.7 22.3 %collective-permute-start.10 = (bf16[64,8192]{1,0:T(8,128)(2,1)S(1)}, bf16[64,8192]{1,0:T(8,128)(2,1)S(1)}, u32[]{:S(2)}, u32[]{:S(2)}) collective-permute-start(bf16[64,8192]{1,0:T(8,128)(2,1)S(1)} %collective-permute-done.9), channel_id=1, source_target_pairs={{0,2},{2,4},{4,6},{6,8},{8,10},{10,12},{12,14},{14,16},{16,18},{18... | collective-permute-start | bytes 3145736 | tf_op jit(solution)/shard_map/ppermute | solution.py:13
  288.1 1.0 copy-start.17
  289.1 22.4 %collective-permute-start.11 = (bf16[64,8192]{1,0:T(8,128)(2,1)S(1)}, bf16[64,8192]{1,0:T(8,128)(2,1)S(1)}, u32[]{:S(2)}, u32[]{:S(2)}) collective-permute-start(bf16[64,8192]{1,0:T(8,128)(2,1)S(1)} %collective-permute-done.10), channel_id=1, source_target_pairs={{0,2},{2,4},{4,6},{6,8},{8,10},{10,12},{12,14},{14,16},{16,18},{18... | collective-permute-start | bytes 3145736 | tf_op jit(solution)/shard_map/ppermute | solution.py:13
  311.4 1.0 copy-start.19
  312.4 22.9 %collective-permute-start.12 = (bf16[64,8192]{1,0:T(8,128)(2,1)S(1)}, bf16[64,8192]{1,0:T(8,128)(2,1)S(1)}, u32[]{:S(2)}, u32[]{:S(2)}) collective-permute-start(bf16[64,8192]{1,0:T(8,128)(2,1)S(1)} %collective-permute-done.11), channel_id=1, source_target_pairs={{0,2},{2,4},{4,6},{6,8},{8,10},{10,12},{12,14},{14,16},{16,18},{18... | collective-permute-start | bytes 3145736 | tf_op jit(solution)/shard_map/ppermute | solution.py:13
  335.3 1.0 copy-start.21
  336.3 24.7 %collective-permute-start.13 = (bf16[64,8192]{1,0:T(8,128)(2,1)S(1)}, bf16[64,8192]{1,0:T(8,128)(2,1)}, u32[]{:S(2)}, u32[]{:S(2)}) collective-permute-start(bf16[64,8192]{1,0:T(8,128)(2,1)S(1)} %collective-permute-done.12), channel_id=1, source_target_pairs={{0,2},{2,4},{4,6},{6,8},{8,10},{10,12},{12,14},{14,16},{16,18},{18... | collective-permute-start | bytes 3145736 | tf_op jit(solution)/shard_map/ppermute | solution.py:13
  361.0 18.7 %collective-permute-start.14 = (bf16[64,8192]{1,0:T(8,128)(2,1)}, bf16[64,8192]{1,0:T(8,128)(2,1)}, u32[]{:S(2)}, u32[]{:S(2)}) collective-permute-start(bf16[64,8192]{1,0:T(8,128)(2,1)} %collective-permute-done.13), channel_id=1, source_target_pairs={{0,2},{2,4},{4,6},{6,8},{8,10},{10,12},{12,14},{14,16},{16,18},{18... | collective-permute-start | bytes 3145736 | tf_op jit(solution)/shard_map/ppermute | solution.py:13
  361.0 57.6 %copy-start.22 = (bf16[64,8192]{1,0:T(8,128)(2,1)S(1)}, bf16[64,8192]{1,0:T(8,128)(2,1)}, u32[]{:S(2)}) copy-start(bf16[64,8192]{1,0:T(8,128)(2,1)} %copy-done.21) | copy-start | bytes 3145732
  361.0 58.6 %copy-start.20 = (bf16[64,8192]{1,0:T(8,128)(2,1)S(1)}, bf16[64,8192]{1,0:T(8,128)(2,1)}, u32[]{:S(2)}) copy-start(bf16[64,8192]{1,0:T(8,128)(2,1)} %copy-done.19) | copy-start | bytes 3145732
  361.0 59.7 %copy-start.18 = (bf16[64,8192]{1,0:T(8,128)(2,1)S(1)}, bf16[64,8192]{1,0:T(8,128)(2,1)}, u32[]{:S(2)}) copy-start(bf16[64,8192]{1,0:T(8,128)(2,1)} %copy-done.17) | copy-start | bytes 3145732
  361.0 60.8 %copy-start.16 = (bf16[64,8192]{1,0:T(8,128)(2,1)S(1)}, bf16[64,8192]{1,0:T(8,128)(2,1)}, u32[]{:S(2)}) copy-start(bf16[64,8192]{1,0:T(8,128)(2,1)} %copy-done.15) | copy-start | bytes 3145732
  361.0 61.8 %copy-start.14 = (bf16[64,8192]{1,0:T(8,128)(2,1)S(1)}, bf16[64,8192]{1,0:T(8,128)(2,1)}, u32[]{:S(2)}) copy-start(bf16[64,8192]{1,0:T(8,128)(2,1)} %copy-done.13) | copy-start | bytes 3145732
  361.0 62.9 %copy-start.12 = (bf16[64,8192]{1,0:T(8,128)(2,1)S(1)}, bf16[64,8192]{1,0:T(8,128)(2,1)}, u32[]{:S(2)}) copy-start(bf16[64,8192]{1,0:T(8,128)(2,1)} %copy-done.11) | copy-start | bytes 3145732
  361.0 64.0 %copy-start.10 = (bf16[64,8192]{1,0:T(8,128)(2,1)S(1)}, bf16[64,8192]{1,0:T(8,128)(2,1)}, u32[]{:S(2)}) copy-start(bf16[64,8192]{1,0:T(8,128)(2,1)} %copy-done.9) | copy-start | bytes 3145732
  361.1 65.0 %copy-start.8 = (bf16[64,8192]{1,0:T(8,128)(2,1)S(1)}, bf16[64,8192]{1,0:T(8,128)(2,1)}, u32[]{:S(2)}) copy-start(bf16[64,8192]{1,0:T(8,128)(2,1)} %copy-done.7) | copy-start | bytes 3145732
  361.1 66.0 %copy-start.6 = (bf16[64,8192]{1,0:T(8,128)(2,1)S(1)}, bf16[64,8192]{1,0:T(8,128)(2,1)}, u32[]{:S(2)}) copy-start(bf16[64,8192]{1,0:T(8,128)(2,1)} %copy-done.5) | copy-start | bytes 3145732
  361.1 67.1 %copy-start.4 = (bf16[64,8192]{1,0:T(8,128)(2,1)S(1)}, bf16[64,8192]{1,0:T(8,128)(2,1)}, u32[]{:S(2)}) copy-start(bf16[64,8192]{1,0:T(8,128)(2,1)} %copy-done.3) | copy-start | bytes 3145732
  361.1 68.2 %copy-start.2 = (bf16[64,8192]{1,0:T(8,128)(2,1)S(1)}, bf16[64,8192]{1,0:T(8,128)(2,1)}, u32[]{:S(2)}) copy-start(bf16[64,8192]{1,0:T(8,128)(2,1)} %copy-done.1) | copy-start | bytes 3145732
  361.1 72.4 %slice-start = ((s8[14680064]{0:T(1024)(128)(4,1)}), s8[4194304]{0:T(1024)(128)(4,1)S(1)}, s32[]{:S(2)}) async-start(s8[14680064]{0:T(1024)(128)(4,1)} %bitcast.1), calls=%async_computation.2 | async-start | bytes 8388608
  398.0 35.5 %slice-start.1 = ((s8[14680064]{0:T(1024)(128)(4,1)}), s8[4194304]{0:T(1024)(128)(4,1)S(1)}, s32[]{:S(2)}) async-start(s8[14680064]{0:T(1024)(128)(4,1)} %bitcast.1), calls=%async_computation.3 | async-start | bytes 8388608
  413.9 19.6 %slice-start.2 = ((s8[14680064]{0:T(1024)(128)(4,1)}), s8[4194304]{0:T(1024)(128)(4,1)S(1)}, s32[]{:S(2)}) async-start(s8[14680064]{0:T(1024)(128)(4,1)} %bitcast.1), calls=%async_computation.4 | async-start | bytes 8388608
  423.9 9.6 %slice-start.3 = ((s8[14680064]{0:T(1024)(128)(4,1)}), s8[2097152]{0:T(1024)(128)(4,1)S(1)}, s32[]{:S(2)}) async-start(s8[14680064]{0:T(1024)(128)(4,1)} %bitcast.1), calls=%async_computation.5 | async-start | bytes 4194304
Sparse Core Ops, SparseCore 0:
  455.4 7.4 reduce-scatter.1
